TPU v7x, 32 devices: a whole 2x2x4 slice. The times are simulated.
32 devices in a mesh: row: 4 (over z), col: 8 (over y, x, core).
Axes of the slice: x: 2, y: 2, z: 4, core: 2. Of those that a mesh axis runs over, the one named last changes fastest.
Arguments:
- weight: float32 [16384, 16384], P('row', 'col'), may hold values from -0.046875 to 0.046875
- leak: float32 [16384], P('col'), may hold values from 0.1 to 1
- rates: float32 [3, 256, 16384], P(None, 'row', 'col'), may hold values from -0.95 to 0.95
- cotangent: float32 [256, 16384], P('row', 'col'), may hold values from -2 to 2
Outputs:
- grad_input: float32 [256, 16384], P('row', 'col')
- grad_weight: float32 [16384, 16384], P('row', 'col')
- grad_noise: float32 [3, 16384], P(None, 'row')
All inputs are finite; a program needn't handle non-finite values.
Results may differ from a plain program's by a relative error of at most 0.0001.
Values sent between devices are 32-bit elements; how exact they have to be, the bound alone decides.
A program may use at most 192 MiB of HBM per device.

v0:
```python
import jax
import jax.numpy as jnp
from jax import lax
from jax.sharding import PartitionSpec as P

TSTEPS = 3


def shards(weight, leak, rates, cotangent):
    n_col = lax.axis_size("col")
    own_rows = cotangent.shape[0]
    local_units = cotangent.shape[1]
    full_rates = lax.all_gather(rates, "row", axis=1, tiled=True)
    grad_weight = jnp.zeros(weight.shape, jnp.float32)
    noise_list = []
    carried = cotangent
    for step_back in range(TSTEPS - 1, -1, -1):
        scaled = leak[None, :] * carried
        spread = scaled.reshape(own_rows, local_units // n_col, n_col)
        by_col = lax.all_to_all(spread, "col", split_axis=2, concat_axis=1, tiled=True)
        by_row = lax.all_to_all(by_col, "row", split_axis=1, concat_axis=0, tiled=True)
        gathered = lax.all_gather(by_row, "col", axis=2, tiled=True)
        unit_block = gathered.reshape(gathered.shape[0], gathered.shape[1] * gathered.shape[2])
        rates_now = full_rates[step_back]
        noise_list.insert(0, jnp.sum(unit_block, axis=0))
        grad_weight = grad_weight + lax.dot_general(
            unit_block,
            rates_now,
            (((0,), (0,)), ((), ())),
            precision=lax.Precision.HIGHEST,
            preferred_element_type=jnp.float32,
        )
        partial_sum = jnp.dot(
            unit_block, weight, precision=lax.Precision.HIGHEST, preferred_element_type=jnp.float32
        )
        adjoint = lax.psum_scatter(partial_sum, "row", scatter_dimension=0, tiled=True)
        local_rates = rates[step_back]
        carried = (1.0 - leak[None, :]) * carried + (1.0 - local_rates * local_rates) * adjoint
    return (carried, grad_weight, jnp.stack(noise_list))


def solution(mesh):
    placed = (P("row", "col"), P("col"), P(None, "row", "col"), P("row", "col"))
    return jax.shard_map(
        shards,
        mesh=mesh,
        in_specs=placed,
        out_specs=(P("row", "col"), P("row", "col"), P(None, "row")),
        check_vma=False,
    )
```

profile of v0, /device:TPU:0, one launch (start us, length us, event | category | flops | bytes accessed | tf_op | source)
XLA Modules:
  0.0 634.5 jit_solution(5892808969612367369)
XLA Ops:
  7.2 1.1 broadcast_multiply_fusion.2
  8.6 0.4 copy.20
  9.0 14.7 %all_to_all.108 = f32[64,256,8]{1,0,2:T(8,128)S(1)} all-to-all(f32[64,256,8]{1,0,2:T(8,128)S(1)} %copy.20), channel_id=1, replica_groups=mesh['row'=4,'col'=8] {'col'}, dimensions={2} | all-to-all | bytes 1048576 | tf_op jit(solution)/shard_map/all_to_all | solution.py:20
  24.1 0.5 broadcast.24
  24.6 9.3 %reduce.3 = f32[2048,64]{1,0:T(8,128)S(1)} reduce(f32[2048,1,64]{2,1,0:T(1,128)S(1)} %bitcast.75, f32[]{:T(128)} %broadcast.24), dimensions={1}, to_apply=%bitcast.64.reduce_sub_computation | reduce | bytes 1048580
  33.9 0.7 reshape.48
  34.6 18.6 %all_to_all.109 = f32[4,1,32768]{2,1,0:T(1,128)S(1)} all-to-all(f32[4,1,32768]{2,1,0:T(1,128)S(1)} %reshape.48), channel_id=1, replica_groups=mesh['row'=4,'col'=8] {'row'}, dimensions={0} | all-to-all | bytes 1048576 | tf_op jit(solution)/shard_map/all_to_all | solution.py:21
  53.2 2.1 reduce.4
  55.3 1.3 reshape.49
  57.0 1.0 copy.24
  58.3 34.2 %all-gather.5.cloned.1.call-done = f32[256,512,8]{1,0,2:T(8,128)} async-done(((f32[256,512,1]{1,0,2:T(8,128)}), f32[256,512,8]{1,0,2:T(8,128)}) %all-gather.5.cloned.1.call-update) | async-done | bytes 4194320 | tf_op jit(solution)/shard_map/all_gather | solution.py:22
  92.6 5.4 copy.25
  98.0 33.9 %fusion.9 = f32[256,2048]{1,0:T(8,128)} fusion(f32[4096,2048]{1,0:T(8,128)} %param.4, f32[256,512,8]{0,2,1:T(8,128)} %copy.25), kind=kOutput, calls=%fused_computation.10 | convolution fusion | flops 25769803776 | bytes 39845888 | tf_op jit(solution)/shard_map/dot_general | solution.py:33
  132.0 43.7 %reduce-scatter.4.cloned.1.call-done = f32[64,2048]{1,0:T(8,128)} async-done(((f32[256,2048]{1,0:T(8,128)}), f32[64,2048]{1,0:T(8,128)}) %reduce-scatter.4.cloned.1.call-update) | async-done | bytes 524304 | tf_op jit(solution)/shard_map/reduce_scatter | solution.py:36
  175.7 1.3 broadcast_multiply_fusion.1
  177.7 13.7 %all_to_all.110 = f32[64,256,8]{1,0,2:T(8,128)S(1)} all-to-all(f32[64,256,8]{1,0,2:T(8,128)S(1)} %copy.27), channel_id=1, replica_groups=mesh['row'=4,'col'=8] {'col'}, dimensions={2} | all-to-all | bytes 1048576 | tf_op jit(solution)/shard_map/all_to_all | solution.py:20
  191.8 9.3 %reduce.5 = f32[2048,64]{1,0:T(8,128)S(1)} reduce(f32[2048,1,64]{2,1,0:T(1,128)S(1)} %bitcast.76, f32[]{:T(128)} %broadcast.24), dimensions={1}, to_apply=%bitcast.66.reduce_sub_computation | reduce | bytes 1048580
  201.1 0.7 reshape.50
  201.8 16.6 %all_to_all.111 = f32[4,1,32768]{2,1,0:T(1,128)S(1)} all-to-all(f32[4,1,32768]{2,1,0:T(1,128)S(1)} %reshape.50), channel_id=1, replica_groups=mesh['row'=4,'col'=8] {'row'}, dimensions={0} | all-to-all | bytes 1048576 | tf_op jit(solution)/shard_map/all_to_all | solution.py:21
  218.4 2.1 reduce.6
  220.5 1.3 reshape.51
  222.2 1.0 copy.31
  223.4 34.3 %all-gather.7.cloned.1.call-done = f32[256,512,8]{1,0,2:T(8,128)} async-done(((f32[256,512,1]{1,0,2:T(8,128)}), f32[256,512,8]{1,0,2:T(8,128)}) %all-gather.7.cloned.1.call-update) | async-done | bytes 4194320 | tf_op jit(solution)/shard_map/all_gather | solution.py:22
  257.7 5.5 copy.32
  263.2 33.8 %fusion.5 = f32[256,2048]{1,0:T(8,128)} fusion(f32[4096,2048]{1,0:T(8,128)} %param.4, f32[256,512,8]{0,2,1:T(8,128)} %copy.32), kind=kOutput, calls=%fused_computation.6 | convolution fusion | flops 25769803776 | bytes 39845888 | tf_op jit(solution)/shard_map/dot_general | solution.py:33
  297.2 0.5 all-gather.11.cloned.1.call-update
  297.8 43.2 %reduce-scatter.6.cloned.1.call-done = f32[64,2048]{1,0:T(8,128)} async-done(((f32[256,2048]{1,0:T(8,128)}), f32[64,2048]{1,0:T(8,128)}) %reduce-scatter.6.cloned.1.call-update) | async-done | bytes 524304 | tf_op jit(solution)/shard_map/reduce_scatter | solution.py:36
  340.9 2.0 broadcast_multiply_fusion
  343.3 0.4 copy.34
  343.7 13.5 %all_to_all.112 = f32[64,256,8]{1,0,2:T(8,128)} all-to-all(f32[64,256,8]{1,0,2:T(8,128)S(1)} %copy.34), channel_id=1, replica_groups=mesh['row'=4,'col'=8] {'col'}, dimensions={2} | all-to-all | bytes 1048576 | tf_op jit(solution)/shard_map/all_to_all | solution.py:20
  357.2 1.4 copy.47
  358.5 10.3 %reduce.7 = f32[2048,64]{1,0:T(8,128)} reduce(f32[2048,1,64]{2,1,0:T(1,128)S(1)} %bitcast.77, f32[]{:T(128)} %broadcast.24), dimensions={1}, to_apply=%bitcast.68.reduce_sub_computation | reduce | bytes 1048580
  368.9 1.9 reshape.52
  370.7 32.0 %all_to_all.113 = f32[4,1,32768]{2,1,0:T(1,128)S(1)} all-to-all(f32[4,1,32768]{2,1,0:T(1,128)S(1)} %reshape.52), channel_id=1, replica_groups=mesh['row'=4,'col'=8] {'row'}, dimensions={0} | all-to-all | bytes 1048576 | tf_op jit(solution)/shard_map/all_to_all | solution.py:21
  402.7 2.1 reduce.8
  404.8 1.3 reshape.53
  406.5 1.0 copy.38
  407.8 2.6 reduce_sum.29
  410.7 57.2 %all-gather.11.cloned.1.call-done = f32[3,256,2048]{2,1,0:T(8,128)} async-done(((f32[3,64,2048]{2,1,0:T(8,128)}), f32[3,256,2048]{2,1,0:T(8,128)}) %all-gather.11.cloned.1.call-update) | async-done | bytes 6291472 | tf_op jit(solution)/shard_map/all_gather | solution.py:13
  468.0 32.4 %fusion.7 = f32[4096,2048]{1,0:T(8,128)} fusion(f32[256,512,8]{0,2,1:T(8,128)} %copy.25, f32[3,256,2048]{2,1,0:T(8,128)} %all-gather.11.cloned.1.call-done), kind=kOutput, calls=%fused_computation.8 | convolution fusion | flops 25769803776 | bytes 39845888 | tf_op jit(solution)/shard_map/dot_general | solution.py:26
  500.4 2.7 reduce_sum.28
  503.4 32.7 %fusion.3 = f32[4096,2048]{1,0:T(8,128)} fusion(f32[256,512,8]{0,2,1:T(8,128)} %copy.32, f32[3,256,2048]{2,1,0:T(8,128)} %all-gather.11.cloned.1.call-done), kind=kOutput, calls=%fused_computation.4 | convolution fusion | flops 25769803776 | bytes 39845888 | tf_op jit(solution)/shard_map/dot_general | solution.py:26
  536.0 2.6 reduce_sum.27
  539.0 5.5 copy.39
  544.4 33.9 %fusion.1 = f32[256,2048]{1,0:T(8,128)} fusion(f32[4096,2048]{1,0:T(8,128)} %param.4, f32[256,512,8]{0,2,1:T(8,128)} %copy.39), kind=kOutput, calls=%fused_computation.2 | convolution fusion | flops 25769803776 | bytes 39845888 | tf_op jit(solution)/shard_map/dot_general | solution.py:33
  578.4 0.7 pad_maximum_fusion
  579.1 46.4 %add_add_fusion = f32[4096,2048]{1,0:T(8,128)} fusion(f32[4096,2048]{1,0:T(8,128)} %fusion.7, f32[4096,2048]{1,0:T(8,128)} %fusion.3, f32[256,512,8]{0,2,1:T(8,128)} %copy.39, f32[3,256,2048]{2,1,0:T(8,128)} %all-gather.11.cloned.1.call-done), kind=kOutput, calls=%fused_computation | convolution fusion | flops 25786580992 | bytes 106954752 | tf_op jit(solution)/shard_map/dot_general | solution.py:26
  625.4 1.9 fusion.11
  (41 shorter events, 5.1 us)
Async XLA Ops:
  7.2 85.4 %all-gather.5.cloned.1.call-start = ((), (), s32[]{:S(2)}) async-start(), calls=%async_computation.9 | async-start | bytes 4718592 | tf_op jit(solution)/shard_map/all_gather | solution.py:22
  58.0 117.7 %reduce-scatter.4.cloned.1.call-start = ((), (), s32[]{:S(2)}) async-start(), calls=%async_computation.10 | async-start | bytes 2621440 | tf_op jit(solution)/shard_map/reduce_scatter | solution.py:36
  98.0 33.9 %copy-start.4 = (f32[2048]{0:T(1024)S(1)}, f32[2048]{0:T(1024)}, u32[]{:S(2)}) copy-start(f32[2048]{0:T(1024)} %param.5) | copy-start | bytes 24580
  98.0 77.7 %copy-start.1 = (f32[64,2048]{1,0:T(8,128)S(1)}, f32[64,2048]{1,0:T(8,128)}, u32[]{:S(2)}) copy-start(f32[64,2048]{1,0:T(8,128)} %param.7) | copy-start | bytes 1572868
  131.9 125.9 %all-gather.7.cloned.1.call-start = ((), (), s32[]{:S(2)}) async-start(), calls=%async_computation.11 | async-start | bytes 4718592 | tf_op jit(solution)/shard_map/all_gather | solution.py:22
  223.2 117.7 %reduce-scatter.6.cloned.1.call-start = ((), (), s32[]{:S(2)}) async-start(), calls=%async_computation.12 | async-start | bytes 2621440 | tf_op jit(solution)/shard_map/reduce_scatter | solution.py:36
  263.2 77.7 %copy-start.3 = (f32[64,2048]{1,0:T(8,128)S(1)}, f32[64,2048]{1,0:T(8,128)}, u32[]{:S(2)}) copy-start(f32[64,2048]{1,0:T(8,128)} %reduce-scatter.4.cloned.1.call-done) | copy-start | bytes 1572868
  297.1 43.8 %copy-start = (f32[3,64,2048]{2,1,0:T(8,128)S(1)}, f32[3,64,2048]{2,1,0:T(8,128)}, u32[]{:S(2)}) copy-start(f32[3,64,2048]{2,1,0:T(8,128)} %param.6) | copy-start | bytes 4718596
  297.1 170.9 %all-gather.11.cloned.1.call-start = ((), (), s32[]{:S(2)}) async-start(), calls=%async_computation.15 | async-start | bytes 7864320 | tf_op jit(solution)/shard_map/all_gather | solution.py:13
  297.7 238.3 %all-gather.9.cloned.1.call-start = ((), (), s32[]{:S(2)}) async-start(), calls=%async_computation.13 | async-start | bytes 4718592 | tf_op jit(solution)/shard_map/all_gather | solution.py:22
  407.5 217.9 %reduce-scatter.8.cloned.1.call-start = ((), (), s32[]{:S(2)}) async-start(), calls=%async_computation.14 | async-start | bytes 2621440 | tf_op jit(solution)/shard_map/reduce_scatter | solution.py:36
  579.1 46.4 %copy-start.2 = (f32[64,2048]{1,0:T(8,128)S(1)}, f32[64,2048]{1,0:T(8,128)}, u32[]{:S(2)}) copy-start(f32[64,2048]{1,0:T(8,128)} %get-tuple-element.4) | copy-start | bytes 1572868
Sparse Core Ops, SparseCore 0:
  58.1 34.4 all-gather.4
  132.0 43.6 reduce-scatter.3
  223.3 34.4 all-gather.6
  297.2 43.6 reduce-scatter.5
  342.3 125.6 all-gather.10
  469.7 34.7 all-gather.8
  578.5 41.7 reduce-scatter.7
where the time goes:
time: 642 us; the launch traced here: 634 us
  waiting for transfers between devices  213 us (33%)
  matrix products  213 us (33%)
  blocking collectives  109 us (17%)
  other arithmetic  50.4 us (8%)
  local copies, waits for them, and re-layouts  33 us (5%)
  between operations  14.6 us (2%)
    dot_general x3, matrix products, shards(): lax.dot_general(unit_block, rates_now, (((0,), (0,)), ((), ())), precisio...  111 us
    dot_general x3, matrix products, shards(): jnp.dot(unit_block, weight, precision=lax.Precision.HIGHEST, preferred_el...  102 us
    reduce_scatter x3, waiting for transfers between devices, shards(): lax.psum_scatter(partial_sum, 'row', scatter_dimension=0, tiled=True)  86.9 us
    all_gather x3, waiting for transfers between devices, shards(): gathered = lax.all_gather(by_row, 'col', axis=2, tiled=True)  68.6 us
    all_to_all x3, blocking collectives, shards(): lax.all_to_all(by_col, 'row', split_axis=1, concat_axis=0, tiled=True)  67.2 us
    all_gather x1, waiting for transfers between devices, shards(): full_rates = lax.all_gather(rates, 'row', axis=1, tiled=True)  57.2 us
    all_to_all x3, blocking collectives, shards(): lax.all_to_all(spread, 'col', split_axis=2, concat_axis=1, tiled=True)  41.9 us
    unnamed x3, other arithmetic  29 us
  transfers between devices with their start and end apart: 7, of which 5 were waited for; matrix products, arithmetic and copies ran while one was open for 22% of the time, Pallas kernels for 0%

commit v1 on v0

--- a/solution.py
+++ b/solution.py
@@ -17,7 +17,12 @@
     for step_back in range(TSTEPS - 1, -1, -1):
         scaled = leak[None, :] * carried
         spread = scaled.reshape(own_rows, local_units // n_col, n_col)
-        by_col = lax.all_to_all(spread, "col", split_axis=2, concat_axis=1, tiled=True)
+        by_col = jnp.concatenate(
+            lax.all_to_all(
+                jnp.stack(jnp.split(spread, lax.axis_size("col"), 2), axis=0), "col", 0, 0
+            ),
+            1,
+        )
         by_row = lax.all_to_all(by_col, "row", split_axis=1, concat_axis=0, tiled=True)
         gathered = lax.all_gather(by_row, "col", axis=2, tiled=True)
         unit_block = gathered.reshape(gathered.shape[0], gathered.shape[1] * gathered.shape[2])

time: 642 us -> 644 us (level)
  no operation moved by 1% of the time
where the time goes in v1:
time: 644 us; the launch traced here: 636 us
  waiting for transfers between devices  213 us (33%)
  matrix products  213 us (33%)
  blocking collectives  109 us (17%)
  other arithmetic  50.4 us (8%)
  local copies, waits for them, and re-layouts  34.2 us (5%)
  between operations  14.9 us (2%)
    dot_general x3, matrix products, shards(): lax.dot_general(unit_block, rates_now, (((0,), (0,)), ((), ())), precisio...  111 us
    dot_general x3, matrix products, shards(): jnp.dot(unit_block, weight, precision=lax.Precision.HIGHEST, preferred_el...  102 us
    reduce_scatter x3, waiting for transfers between devices, shards(): lax.psum_scatter(partial_sum, 'row', scatter_dimension=0, tiled=True)  86.9 us
    all_gather x3, waiting for transfers between devices, shards(): gathered = lax.all_gather(by_row, 'col', axis=2, tiled=True)  68.3 us
    all_to_all x3, blocking collectives, shards(): lax.all_to_all(by_col, 'row', split_axis=1, concat_axis=0, tiled=True)  67.3 us
    all_gather x1, waiting for transfers between devices, shards(): full_rates = lax.all_gather(rates, 'row', axis=1, tiled=True)  57.2 us
    all_to_all x3, blocking collectives, shards(): lax.all_to_all(jnp.stack(jnp.split(spread, lax.axis_size('col'), 2), axis...  41.5 us
    unnamed x3, other arithmetic  29 us
  transfers between devices with their start and end apart: 7, of which 5 were waited for; matrix products, arithmetic and copies ran while one was open for 22% of the time, Pallas kernels for 0%

profile of v1, /device:TPU:0, one launch (start us, length us, event | category | flops | bytes accessed | tf_op | source)
XLA Modules:
  0.0 635.5 jit_solution(4584358490398067704)
XLA Ops:
  7.2 1.1 broadcast_multiply_fusion.2
  8.6 0.7 fusion.17
  9.8 14.7 %all_to_all.69 = f32[8,64,256,1]{2,1,3,0:T(8,128)S(1)} all-to-all(f32[8,64,256,1]{2,1,3,0:T(8,128)S(1)} %copy.73), channel_id=1, replica_groups=mesh['row'=4,'col'=8] {'col'}, dimensions={0} | all-to-all | bytes 1048576 | tf_op jit(solution)/shard_map/all_to_all | solution.py:21
  25.4 9.3 %reduce.3 = f32[2048,64]{1,0:T(8,128)S(1)} reduce(f32[2048,1,64]{2,1,0:T(1,128)S(1)} %bitcast.129, f32[]{:T(128)} %broadcast.24), dimensions={1}, to_apply=%bitcast.118.reduce_sub_computation | reduce | bytes 1048580
  34.7 0.7 reshape.72
  35.4 18.6 %all_to_all.70 = f32[4,1,32768]{2,1,0:T(1,128)S(1)} all-to-all(f32[4,1,32768]{2,1,0:T(1,128)S(1)} %reshape.72), channel_id=1, replica_groups=mesh['row'=4,'col'=8] {'row'}, dimensions={0} | all-to-all | bytes 1048576 | tf_op jit(solution)/shard_map/all_to_all | solution.py:26
  54.0 2.1 reduce.4
  56.1 1.3 reshape.73
  57.8 1.0 copy.77
  58.8 0.6 reduce-scatter.4.cloned.1.call-start
  59.4 34.0 %all-gather.5.cloned.1.call-done = f32[256,512,8]{1,0,2:T(8,128)} async-done(((f32[256,512,1]{1,0,2:T(8,128)}), f32[256,512,8]{1,0,2:T(8,128)}) %all-gather.5.cloned.1.call-update) | async-done | bytes 4194320 | tf_op jit(solution)/shard_map/all_gather | solution.py:27
  93.4 5.4 copy.78
  98.8 33.9 %fusion.9 = f32[256,2048]{1,0:T(8,128)} fusion(f32[4096,2048]{1,0:T(8,128)} %param.4, f32[256,512,8]{0,2,1:T(8,128)} %copy.78), kind=kOutput, calls=%fused_computation.10 | convolution fusion | flops 25769803776 | bytes 39845888 | tf_op jit(solution)/shard_map/dot_general | solution.py:38
  132.8 43.7 %reduce-scatter.4.cloned.1.call-done = f32[64,2048]{1,0:T(8,128)} async-done(((f32[256,2048]{1,0:T(8,128)}), f32[64,2048]{1,0:T(8,128)}) %reduce-scatter.4.cloned.1.call-update) | async-done | bytes 524304 | tf_op jit(solution)/shard_map/reduce_scatter | solution.py:41
  176.5 1.3 broadcast_multiply_fusion.1
  178.1 0.7 fusion.16
  179.3 13.3 %all_to_all.71 = f32[8,64,256,1]{2,1,3,0:T(8,128)S(1)} all-to-all(f32[8,64,256,1]{2,1,3,0:T(8,128)S(1)} %copy.88), channel_id=1, replica_groups=mesh['row'=4,'col'=8] {'col'}, dimensions={0} | all-to-all | bytes 1048576 | tf_op jit(solution)/shard_map/all_to_all | solution.py:21
  193.0 9.3 %reduce.5 = f32[2048,64]{1,0:T(8,128)S(1)} reduce(f32[2048,1,64]{2,1,0:T(1,128)S(1)} %bitcast.130, f32[]{:T(128)} %broadcast.24), dimensions={1}, to_apply=%bitcast.120.reduce_sub_computation | reduce | bytes 1048580
  202.4 0.7 reshape.74
  203.0 16.6 %all_to_all.72 = f32[4,1,32768]{2,1,0:T(1,128)S(1)} all-to-all(f32[4,1,32768]{2,1,0:T(1,128)S(1)} %reshape.74), channel_id=1, replica_groups=mesh['row'=4,'col'=8] {'row'}, dimensions={0} | all-to-all | bytes 1048576 | tf_op jit(solution)/shard_map/all_to_all | solution.py:26
  219.6 2.1 reduce.6
  221.8 1.3 reshape.75
  223.4 1.0 copy.92
  224.7 34.3 %all-gather.7.cloned.1.call-done = f32[256,512,8]{1,0,2:T(8,128)} async-done(((f32[256,512,1]{1,0,2:T(8,128)}), f32[256,512,8]{1,0,2:T(8,128)}) %all-gather.7.cloned.1.call-update) | async-done | bytes 4194320 | tf_op jit(solution)/shard_map/all_gather | solution.py:27
  259.0 5.5 copy.93
  264.5 33.9 %fusion.5 = f32[256,2048]{1,0:T(8,128)} fusion(f32[4096,2048]{1,0:T(8,128)} %param.4, f32[256,512,8]{0,2,1:T(8,128)} %copy.93), kind=kOutput, calls=%fused_computation.6 | convolution fusion | flops 25769803776 | bytes 39845888 | tf_op jit(solution)/shard_map/dot_general | solution.py:38
  298.4 0.5 all-gather.11.cloned.1.call-update
  299.0 43.2 %reduce-scatter.6.cloned.1.call-done = f32[64,2048]{1,0:T(8,128)} async-done(((f32[256,2048]{1,0:T(8,128)}), f32[64,2048]{1,0:T(8,128)}) %reduce-scatter.6.cloned.1.call-update) | async-done | bytes 524304 | tf_op jit(solution)/shard_map/reduce_scatter | solution.py:41
  342.2 2.0 broadcast_multiply_fusion
  344.5 0.7 fusion.15
  345.7 13.4 %all_to_all.73 = f32[8,64,256,1]{2,1,3,0:T(8,128)S(1)} all-to-all(f32[8,64,256,1]{2,1,3,0:T(8,128)S(1)} %copy.103), channel_id=1, replica_groups=mesh['row'=4,'col'=8] {'col'}, dimensions={0} | all-to-all | bytes 1048576 | tf_op jit(solution)/shard_map/all_to_all | solution.py:21
  359.5 10.3 %reduce.7 = f32[2048,64]{1,0:T(8,128)} reduce(f32[2048,1,64]{2,1,0:T(1,128)S(1)} %bitcast.131, f32[]{:T(128)} %broadcast.24), dimensions={1}, to_apply=%bitcast.122.reduce_sub_computation | reduce | bytes 1048580
  369.8 1.9 reshape.76
  371.7 32.1 %all_to_all.74 = f32[4,1,32768]{2,1,0:T(1,128)S(1)} all-to-all(f32[4,1,32768]{2,1,0:T(1,128)S(1)} %reshape.76), channel_id=1, replica_groups=mesh['row'=4,'col'=8] {'row'}, dimensions={0} | all-to-all | bytes 1048576 | tf_op jit(solution)/shard_map/all_to_all | solution.py:26
  403.7 2.1 reduce.8
  405.9 1.3 reshape.77
  407.6 1.0 copy.107
  409.1 2.6 reduce_sum.29
  412.0 57.2 %all-gather.11.cloned.1.call-done = f32[3,256,2048]{2,1,0:T(8,128)} async-done(((f32[3,64,2048]{2,1,0:T(8,128)}), f32[3,256,2048]{2,1,0:T(8,128)}) %all-gather.11.cloned.1.call-update) | async-done | bytes 6291472 | tf_op jit(solution)/shard_map/all_gather | solution.py:13
  469.2 32.4 %fusion.7 = f32[4096,2048]{1,0:T(8,128)} fusion(f32[256,512,8]{0,2,1:T(8,128)} %copy.78, f32[3,256,2048]{2,1,0:T(8,128)} %all-gather.11.cloned.1.call-done), kind=kOutput, calls=%fused_computation.8 | convolution fusion | flops 25769803776 | bytes 39845888 | tf_op jit(solution)/shard_map/dot_general | solution.py:31
  501.6 2.7 reduce_sum.28
  504.6 32.4 %fusion.3 = f32[4096,2048]{1,0:T(8,128)} fusion(f32[256,512,8]{0,2,1:T(8,128)} %copy.93, f32[3,256,2048]{2,1,0:T(8,128)} %all-gather.11.cloned.1.call-done), kind=kOutput, calls=%fused_computation.4 | convolution fusion | flops 25769803776 | bytes 39845888 | tf_op jit(solution)/shard_map/dot_general | solution.py:31
  537.0 2.6 reduce_sum.27
  539.9 5.5 copy.108
  545.4 34.0 %fusion.1 = f32[256,2048]{1,0:T(8,128)} fusion(f32[4096,2048]{1,0:T(8,128)} %param.4, f32[256,512,8]{0,2,1:T(8,128)} %copy.108), kind=kOutput, calls=%fused_computation.2 | convolution fusion | flops 25769803776 | bytes 39845888 | tf_op jit(solution)/shard_map/dot_general | solution.py:38
  579.4 0.7 pad_maximum_fusion
  580.1 46.4 %add_add_fusion = f32[4096,2048]{1,0:T(8,128)} fusion(f32[4096,2048]{1,0:T(8,128)} %fusion.7, f32[4096,2048]{1,0:T(8,128)} %fusion.3, f32[256,512,8]{0,2,1:T(8,128)} %copy.108, f32[3,256,2048]{2,1,0:T(8,128)} %all-gather.11.cloned.1.call-done), kind=kOutput, calls=%fused_computation | convolution fusion | flops 25786580992 | bytes 106954752 | tf_op jit(solution)/shard_map/dot_general | solution.py:31
  626.5 1.9 fusion.11
  (68 shorter events, 6.8 us)
Async XLA Ops:
  7.2 86.2 %all-gather.5.cloned.1.call-start = ((), (), s32[]{:S(2)}) async-start(), calls=%async_computation.9 | async-start | bytes 4718592 | tf_op jit(solution)/shard_map/all_gather | solution.py:27
  58.8 117.7 %reduce-scatter.4.cloned.1.call-start = ((), (), s32[]{:S(2)}) async-start(), calls=%async_computation.10 | async-start | bytes 2621440 | tf_op jit(solution)/shard_map/reduce_scatter | solution.py:41
  98.8 33.9 %copy-start.4 = (f32[2048]{0:T(1024)S(1)}, f32[2048]{0:T(1024)}, u32[]{:S(2)}) copy-start(f32[2048]{0:T(1024)} %param.5) | copy-start | bytes 24580
  98.8 77.7 %copy-start.1 = (f32[64,2048]{1,0:T(8,128)S(1)}, f32[64,2048]{1,0:T(8,128)}, u32[]{:S(2)}) copy-start(f32[64,2048]{1,0:T(8,128)} %param.7) | copy-start | bytes 1572868
  132.7 126.3 %all-gather.7.cloned.1.call-start = ((), (), s32[]{:S(2)}) async-start(), calls=%async_computation.11 | async-start | bytes 4718592 | tf_op jit(solution)/shard_map/all_gather | solution.py:27
  224.4 117.7 %reduce-scatter.6.cloned.1.call-start = ((), (), s32[]{:S(2)}) async-start(), calls=%async_computation.12 | async-start | bytes 2621440 | tf_op jit(solution)/shard_map/reduce_scatter | solution.py:41
  264.5 77.7 %copy-start.3 = (f32[64,2048]{1,0:T(8,128)S(1)}, f32[64,2048]{1,0:T(8,128)}, u32[]{:S(2)}) copy-start(f32[64,2048]{1,0:T(8,128)} %reduce-scatter.4.cloned.1.call-done) | copy-start | bytes 1572868
  298.3 43.8 %copy-start = (f32[3,64,2048]{2,1,0:T(8,128)S(1)}, f32[3,64,2048]{2,1,0:T(8,128)}, u32[]{:S(2)}) copy-start(f32[3,64,2048]{2,1,0:T(8,128)} %param.6) | copy-start | bytes 4718596
  298.4 170.9 %all-gather.11.cloned.1.call-start = ((), (), s32[]{:S(2)}) async-start(), calls=%async_computation.15 | async-start | bytes 7864320 | tf_op jit(solution)/shard_map/all_gather | solution.py:13
  299.0 238.0 %all-gather.9.cloned.1.call-start = ((), (), s32[]{:S(2)}) async-start(), calls=%async_computation.13 | async-start | bytes 4718592 | tf_op jit(solution)/shard_map/all_gather | solution.py:27
  408.6 217.9 %reduce-scatter.8.cloned.1.call-start = ((), (), s32[]{:S(2)}) async-start(), calls=%async_computation.14 | async-start | bytes 2621440 | tf_op jit(solution)/shard_map/reduce_scatter | solution.py:41
  580.1 46.4 %copy-start.2 = (f32[64,2048]{1,0:T(8,128)S(1)}, f32[64,2048]{1,0:T(8,128)}, u32[]{:S(2)}) copy-start(f32[64,2048]{1,0:T(8,128)} %get-tuple-element.4) | copy-start | bytes 1572868
Sparse Core Ops, SparseCore 0:
  58.9 34.4 all-gather.4
  132.8 43.6 reduce-scatter.3
  224.5 34.4 all-gather.6
  298.5 43.6 reduce-scatter.5
  343.6 125.6 all-gather.10
  471.0 34.7 all-gather.8
  579.5 41.7 reduce-scatter.7
